TPU v7x, 256 devices: a whole 4x4x8 slice. The times are simulated.
256 devices in a mesh: feat: 16 (over z, core), dom: 16 (over x, y).
Axes of the slice: x: 4, y: 4, z: 8, core: 2. Of those that a mesh axis runs over, the one named last changes fastest.
Arguments:
- features: bfloat16 [16, 1024, 9216], P('dom', 'feat'), may hold values from -6 to 6
- w1_self: bfloat16 [1024, 256], P('feat'), may hold values from -0.1875 to 0.1875
- w1_neigh: bfloat16 [1024, 256], P('feat'), may hold values from -0.1875 to 0.1875
- w2_self: bfloat16 [256, 256], replicated, may hold values from -0.375 to 0.375
- w2_neigh: bfloat16 [256, 256], replicated, may hold values from -0.375 to 0.375
- neigh_one: int32 [16, 10, 4608], P('dom'), may hold values from 0 to 9215
- send_rows: int32 [16, 16, 16, 128], P('dom', 'feat'), may hold values from 0 to 287
- recv_count: int32 [16, 16, 16], P(None, 'feat', 'dom'), may hold values from 1 to 128, as said below
- neigh_two: int32 [16, 16, 256, 15], P('dom', 'feat'), may hold values from 0 to 2047, as said below
- seed_rows: int32 [16, 16, 256], P('dom', 'feat'), may hold values from 0 to 287, as said below
- d_out: bfloat16 [16, 16, 256, 256], P('dom', 'feat'), may hold values from -0.0625 to 0.0625
Outputs:
- layer_two: bfloat16 [16, 16, 256, 256], P('dom', 'feat')
- grad_w1_self: float32 [1024, 256], P('feat')
- grad_w1_neigh: float32 [1024, 256], P('feat')
- grad_w2_self: float32 [256, 256], replicated
- grad_w2_neigh: float32 [256, 256], replicated
Inputs may be any that keep to these rules, and one draw needn't show every extreme that they name: `neigh_one`: columns of the partition's 9216 input nodes. `send_rows`: rows among the sending device's 288 owned nodes. `recv_count`: the live slots of a buffer are its leading ones; every receiver gets a full buffer of 128 live rows from some source, and some receiver gets full buffers from every source. `neigh_two`: each is below the total of the receiving device's counts; on every device some seed names the last live row. `seed_rows`: distinct within one device.
All inputs are finite; a program needn't handle non-finite values.
Results may differ from a plain program's by a relative error of at most 0.0051.
Values may be sent and summed in bfloat16 or wider, within the bound.
No kernel may reach another device: no remote copies, remote signals or barrier semaphores. Data moves between devices by JAX's collectives and lax.ppermute only.
A program may use at most 64 MiB of HBM per device.

v0:
```python
import jax
import jax.numpy as jnp
from jax import lax
from jax.sharding import PartitionSpec as P


def rows_of(source_table, index_rows):
    return jnp.take(source_table, index_rows, axis=0)


def contract_rows(left_side, right_side):
    return lax.dot_general(
        left_side, right_side, (((0,), (0,)), ((), ())), preferred_element_type=jnp.float32
    )


def contract_cols(left_side, right_side):
    return lax.dot_general(
        left_side, right_side, (((1,), (1,)), ((), ())), preferred_element_type=jnp.float32
    )


def per_device(
    features,
    w1_self,
    w1_neigh,
    w2_self,
    w2_neigh,
    neigh_one,
    send_rows,
    recv_count,
    neigh_two,
    seed_rows,
    d_out,
):
    feature_table = features[0]
    neigh_lists = neigh_one[0]
    target_rows = neigh_lists.shape[1]
    fan_one = neigh_lists.shape[0]
    running = jnp.zeros((feature_table.shape[0], target_rows), jnp.float32)
    for column in range(fan_one):
        running = running + jnp.take(feature_table, neigh_lists[column], axis=1).astype(jnp.float32)
    mean_one = (running / fan_one).astype(jnp.bfloat16)
    own_self = feature_table[:, :target_rows]
    owned_rows = target_rows // lax.axis_size("feat")
    hidden_width = w1_self.shape[1]
    left_self = own_self
    left_mean = mean_one
    pre_one = lax.psum_scatter(
        contract_rows(left_self, w1_self) + contract_rows(left_mean, w1_neigh),
        "feat",
        scatter_dimension=0,
        tiled=True,
    )
    hidden = jax.nn.elu(pre_one).astype(jnp.bfloat16)
    send_index = send_rows[0, 0]
    peer_count = send_index.shape[0]
    slot_count = send_index.shape[1]
    outgoing = rows_of(hidden, send_index.reshape(-1)).reshape(peer_count, slot_count, hidden_width)
    incoming = lax.all_to_all(outgoing, "dom", split_axis=0, concat_axis=0, tiled=True)
    flat_in = incoming.reshape(peer_count * slot_count, hidden_width)
    counts = recv_count[:, 0, 0]
    starts = jnp.cumsum(counts) - counts
    positions = neigh_two[0, 0]
    source = jnp.sum((positions[:, :, None] >= starts[None, None, 1:]).astype(jnp.int32), axis=2)
    picked = (source[:, :, None] == jnp.arange(peer_count, dtype=jnp.int32)).astype(jnp.int32)
    offset_of = jnp.sum(picked * starts[None, None, :], axis=2)
    where_in = source * slot_count + positions - offset_of
    fan_two = positions.shape[1]
    seed_count = positions.shape[0]
    running_two = jnp.zeros((seed_count, hidden_width), jnp.float32)
    for column in range(fan_two):
        running_two = running_two + rows_of(flat_in, where_in[:, column]).astype(jnp.float32)
    mean_two = (running_two / fan_two).astype(jnp.bfloat16)
    seeds = seed_rows[0, 0]
    self_two = rows_of(hidden, seeds)
    grad_out = d_out[0, 0]
    layer_out = (
        jnp.dot(self_two, w2_self, preferred_element_type=jnp.float32)
        + jnp.dot(mean_two, w2_neigh, preferred_element_type=jnp.float32)
    ).astype(jnp.bfloat16)
    local_w2_self = contract_rows(self_two, grad_out)
    local_w2_neigh = contract_rows(mean_two, grad_out)
    d_self = contract_cols(grad_out, w2_self)
    d_mean = contract_cols(grad_out, w2_neigh) / fan_two
    slot_sum = jnp.zeros((peer_count * slot_count, hidden_width), jnp.float32)
    for column in range(fan_two):
        slot_sum = slot_sum.at[where_in[:, column]].add(d_mean)
    slot_grad = slot_sum.astype(jnp.bfloat16).reshape(peer_count, slot_count, hidden_width)
    returned = lax.all_to_all(slot_grad, "dom", split_axis=0, concat_axis=0, tiled=True)
    d_hidden = jnp.zeros((owned_rows, hidden_width), jnp.float32)
    d_hidden = d_hidden.at[send_index.reshape(-1)].add(
        returned.reshape(-1, hidden_width).astype(jnp.float32)
    )
    d_hidden = d_hidden.at[seeds].add(d_self)
    elu_slope = jnp.where(pre_one > 0, 1.0, jnp.exp(jnp.minimum(pre_one, 0.0)))
    d_pre = (d_hidden * elu_slope).astype(jnp.bfloat16)
    piece = lax.all_gather(d_pre, "feat", axis=0, tiled=True)
    left_self = own_self
    left_mean = mean_one
    first_self = jnp.dot(left_self, piece, preferred_element_type=jnp.float32)
    first_mean = jnp.dot(left_mean, piece, preferred_element_type=jnp.float32)
    first_self, first_mean = lax.psum((first_self, first_mean), "dom")
    second_self, second_mean = lax.psum((local_w2_self, local_w2_neigh), ("feat", "dom"))
    return (layer_out[None, None], first_self, first_mean, second_self, second_mean)


def solution(mesh):
    return jax.shard_map(
        per_device,
        mesh=mesh,
        in_specs=(
            P("dom", "feat", None),
            P("feat", None),
            P("feat", None),
            P(),
            P(),
            P("dom", None, None),
            P("dom", "feat", None, None),
            P(None, "feat", "dom"),
            P("dom", "feat", None, None),
            P("dom", "feat", None),
            P("dom", "feat", None, None),
        ),
        out_specs=(P("dom", "feat", None, None), P("feat", None), P("feat", None), P(), P()),
        check_vma=False,
    )
```

profile of v0, /device:TPU:2, one launch (start us, length us, event | category | flops | bytes accessed | tf_op | source)
XLA Modules:
  0.0 690.3 jit_solution(7600817708877585368)
XLA Ops:
  11.5 10.1 %gather_fusion.2 = bf16[4608,64]{1,0:T(8,128)(2,1)} fusion(bf16[64,9216]{0,1:T(8,128)(2,1)S(1)} %bitcast.99, s32[5120]{0:T(1024)S(1)} %pad_clamp_fusion.9), kind=kCustom, calls=%fused_computation.clone | custom fusion | bytes 1198080 | tf_op jit(solution)/shard_map/jit(_take)/gather | solution.py:42
  21.6 10.1 %gather_fusion.3 = bf16[4608,64]{1,0:T(8,128)(2,1)} fusion(bf16[64,9216]{0,1:T(8,128)(2,1)S(1)} %bitcast.100, s32[5120]{0:T(1024)S(1)} %pad_clamp_fusion.8), kind=kCustom, calls=%fused_computation.2.clone | custom fusion | bytes 1198080 | tf_op jit(solution)/shard_map/jit(_take)/gather | solution.py:42
  31.7 10.1 %gather_fusion.4 = bf16[4608,64]{1,0:T(8,128)(2,1)} fusion(bf16[64,9216]{0,1:T(8,128)(2,1)S(1)} %bitcast.101, s32[5120]{0:T(1024)S(1)} %pad_clamp_fusion.7), kind=kCustom, calls=%fused_computation.3.clone | custom fusion | bytes 1198080 | tf_op jit(solution)/shard_map/jit(_take)/gather | solution.py:42
  41.8 10.1 %gather_fusion.5 = bf16[4608,64]{1,0:T(8,128)(2,1)} fusion(bf16[64,9216]{0,1:T(8,128)(2,1)S(1)} %bitcast.102, s32[5120]{0:T(1024)S(1)} %pad_clamp_fusion.6), kind=kCustom, calls=%fused_computation.4.clone | custom fusion | bytes 1198080 | tf_op jit(solution)/shard_map/jit(_take)/gather | solution.py:42
  51.9 10.1 %gather_fusion.6 = bf16[4608,64]{1,0:T(8,128)(2,1)} fusion(bf16[64,9216]{0,1:T(8,128)(2,1)S(1)} %bitcast.103, s32[5120]{0:T(1024)S(1)} %pad_clamp_fusion.5), kind=kCustom, calls=%fused_computation.5.clone | custom fusion | bytes 1198080 | tf_op jit(solution)/shard_map/jit(_take)/gather | solution.py:42
  62.1 10.1 %gather_fusion.7 = bf16[4608,64]{1,0:T(8,128)(2,1)} fusion(bf16[64,9216]{0,1:T(8,128)(2,1)S(1)} %bitcast.104, s32[5120]{0:T(1024)S(1)} %pad_clamp_fusion.4), kind=kCustom, calls=%fused_computation.6.clone | custom fusion | bytes 1198080 | tf_op jit(solution)/shard_map/jit(_take)/gather | solution.py:42
  72.2 10.1 %gather_fusion.8 = bf16[4608,64]{1,0:T(8,128)(2,1)} fusion(bf16[64,9216]{0,1:T(8,128)(2,1)S(1)} %bitcast.105, s32[5120]{0:T(1024)S(1)} %pad_clamp_fusion.3), kind=kCustom, calls=%fused_computation.7.clone | custom fusion | bytes 1198080 | tf_op jit(solution)/shard_map/jit(_take)/gather | solution.py:42
  82.3 10.1 %gather_fusion.9 = bf16[4608,64]{1,0:T(8,128)(2,1)} fusion(bf16[64,9216]{0,1:T(8,128)(2,1)S(1)} %bitcast.106, s32[5120]{0:T(1024)S(1)} %pad_clamp_fusion.2), kind=kCustom, calls=%fused_computation.8.clone | custom fusion | bytes 1198080 | tf_op jit(solution)/shard_map/jit(_take)/gather | solution.py:42
  92.4 10.1 %gather_fusion.10 = bf16[4608,64]{1,0:T(8,128)(2,1)} fusion(bf16[64,9216]{0,1:T(8,128)(2,1)S(1)} %bitcast.107, s32[5120]{0:T(1024)S(1)} %pad_clamp_fusion.1), kind=kCustom, calls=%fused_computation.9.clone | custom fusion | bytes 1198080 | tf_op jit(solution)/shard_map/jit(_take)/gather | solution.py:42
  102.6 10.1 %gather_fusion.11 = bf16[4608,64]{1,0:T(8,128)(2,1)} fusion(bf16[64,9216]{0,1:T(8,128)(2,1)S(1)} %bitcast.108, s32[5120]{0:T(1024)S(1)} %pad_clamp_fusion), kind=kCustom, calls=%fused_computation.10.clone | custom fusion | bytes 1198080 | tf_op jit(solution)/shard_map/jit(_take)/gather | solution.py:42
  116.8 10.3 %multiply_convert_fusion = bf16[64,4608]{0,1:T(8,128)(2,1)S(1)} fusion(bf16[4608,64]{1,0:T(8,128)(2,1)} %gather_fusion.11, bf16[4608,64]{1,0:T(8,128)(2,1)S(1)} %copy-done.11, bf16[4608,64]{1,0:T(8,128)(2,1)S(1)} %copy-done.10, bf16[4608,64]{1,0:T(8,128)(2,1)S(1)} %copy-done.9, bf16[4608,64]{1,0:T(8,128)(2,1)S(1)} %copy-done.8, ...), kind=kLoop, calls=%fused_computation.45 | loop fusion | flops 9142272 | bytes 6534144 | tf_op jit(solution)/shard_map/convert_element_type | solution.py:43
  141.2 5.2 scatter_fusion.1
  151.1 4.8 scatter_fusion.3
  165.3 4.8 scatter_fusion.6
  170.1 4.8 scatter_fusion.7
  184.3 4.8 scatter_fusion.10
  189.1 4.9 scatter_fusion.11
  206.2 7.5 %all-to-all-start.1 = ((bf16[16,128,256]{2,1,0:T(8,128)(2,1)}), bf16[16,128,256]{2,1,0:T(8,128)(2,1)S(1)}, u32[]{:S(2)}, u32[]{:S(2)}) async-start(bf16[16,128,256]{2,1,0:T(8,128)(2,1)} %bitcast.53), calls=%async_computation.2 | async-start | bytes 2097152 | tf_op jit(solution)/shard_map/all_to_all | solution.py:90
  229.7 11.0 %scatter_custom_fusion.15 = f32[288,256]{1,0:T(8,128)S(1)} fusion(s32[2048]{0:T(1024)S(1)} %bitcast.115, bf16[2048,256]{1,0:T(8,128)(2,1)} %bitcast.111, f32[]{:T(128)} %constant.47.clone.1), kind=kCustom, calls=%fused_computation.46 | custom fusion | flops 1048576 | bytes 1343492 | tf_op jit(solution)/shard_map/scatter-add | solution.py:92
  249.9 9.0 %gather_fusion.1 = bf16[2048,256]{1,0:T(8,128)(2,1)} fusion(bf16[288,256]{1,0:T(8,128)(2,1)S(1)} %get-tuple-element.22, s32[2048]{0:T(1024)S(1)} %broadcast_clamp_fusion), kind=kCustom, calls=%fused_computation.26 | custom fusion | bytes 2105344 | tf_op jit(solution)/shard_map/jit(_take)/gather | solution.py:8
  261.2 7.0 %all-to-all-start = ((bf16[16,128,256]{2,1,0:T(8,128)(2,1)}), bf16[16,128,256]{2,1,0:T(8,128)(2,1)}, u32[]{:S(2)}, u32[]{:S(2)}) async-start(bf16[16,128,256]{2,1,0:T(8,128)(2,1)} %broadcast_select_fusion), calls=%async_computation.1 | async-start | bytes 2097152 | tf_op jit(solution)/shard_map/all_to_all | solution.py:60
  272.5 10.3 %all-to-all-done = bf16[16,128,256]{2,1,0:T(8,128)(2,1)} async-done(((bf16[16,128,256]{2,1,0:T(8,128)(2,1)}), bf16[16,128,256]{2,1,0:T(8,128)(2,1)}, u32[]{:S(2)}, u32[]{:S(2)}) %all-to-all-start) | async-done | bytes 1048608 | tf_op jit(solution)/shard_map/all_to_all | solution.py:60
  334.9 247.9 %all-reduce.5.cloned.1.call-done = (f32[256,256]{1,0:T(8,128)}, f32[256,256]{1,0:T(8,128)}) async-done(((f32[256,256]{1,0:T(8,128)}, f32[256,256]{1,0:T(8,128)}), (f32[256,256]{1,0:T(8,128)}, f32[256,256]{1,0:T(8,128)})) %all-reduce.5.cloned.1.call-update) | async-done | bytes 524304 | tf_op jit(solution)/shard_map/psum | solution.py:104
  582.8 94.5 %all-reduce.7.cloned.1.call-done = (f32[64,256]{1,0:T(8,128)}, f32[64,256]{1,0:T(8,128)}) async-done(((f32[64,256]{1,0:T(8,128)}, f32[64,256]{1,0:T(8,128)}), (f32[64,256]{1,0:T(8,128)}, f32[64,256]{1,0:T(8,128)})) %all-reduce.7.cloned.1.call-update) | async-done | bytes 131088 | tf_op jit(solution)/shard_map/psum | solution.py:103
  (234 shorter events, 148.0 us)
Async XLA Ops:
  7.2 125.6 %copy-start = (bf16[1,1,256,256]{3,2,1,0:T(8,128)(2,1)S(1)}, bf16[1,1,256,256]{3,2,1,0:T(8,128)(2,1)}, u32[]{:S(2)}) copy-start(bf16[1,1,256,256]{3,2,1,0:T(8,128)(2,1)} %param.25) | copy-start | bytes 393220
  7.2 236.3 %reduce-scatter.2.cloned.1.call-start = ((), (), s32[]{:S(2)}) async-start(), calls=%async_computation.3 | async-start | bytes 5013504 | tf_op jit(solution)/shard_map/reduce_scatter | solution.py:49
  102.5 10.1 %copy-start.17 = (bf16[64,256]{1,0:T(8,128)(2,1)S(1)}, bf16[64,256]{1,0:T(8,128)(2,1)}, u32[]{:S(2)}) copy-start(bf16[64,256]{1,0:T(8,128)(2,1)} %param.16) | copy-start | bytes 98308
  116.7 11.3 %copy-start.18 = (bf16[64,256]{1,0:T(8,128)(2,1)S(1)}, bf16[64,256]{1,0:T(8,128)(2,1)}, u32[]{:S(2)}) copy-start(bf16[64,256]{1,0:T(8,128)(2,1)} %param.17) | copy-start | bytes 98308
  206.2 22.5 %all-to-all-start.1 = ((bf16[16,128,256]{2,1,0:T(8,128)(2,1)}), bf16[16,128,256]{2,1,0:T(8,128)(2,1)S(1)}, u32[]{:S(2)}, u32[]{:S(2)}) async-start(bf16[16,128,256]{2,1,0:T(8,128)(2,1)} %bitcast.53), calls=%async_computation.2 | async-start | bytes 2097152 | tf_op jit(solution)/shard_map/all_to_all | solution.py:90
  213.7 115.7 %all-gather.2.cloned.1.call-start = ((), (), s32[]{:S(2)}) async-start(), calls=%async_computation.4 | async-start | bytes 2506752 | tf_op jit(solution)/shard_map/all_gather | solution.py:98
  219.4 8.0 %copy-start.32 = (s32[256,1]{0,1:T(1,128)}, s32[256,1]{0,1:T(1,128)S(1)}, u32[]{:S(2)}) copy-start(s32[256,1]{0,1:T(1,128)S(1)} %get-tuple-element.47) | copy-start | bytes 3076
  219.4 8.0 %copy-start.34 = (s32[256,1]{0,1:T(1,128)}, s32[256,1]{0,1:T(1,128)S(1)}, u32[]{:S(2)}) copy-start(s32[256,1]{0,1:T(1,128)S(1)} %get-tuple-element.48) | copy-start | bytes 3076
  219.4 8.0 %copy-start.36 = (s32[256,1]{0,1:T(1,128)}, s32[256,1]{0,1:T(1,128)S(1)}, u32[]{:S(2)}) copy-start(s32[256,1]{0,1:T(1,128)S(1)} %get-tuple-element.45) | copy-start | bytes 3076
  240.9 8.5 %copy-start.33 = (s32[256,1]{0,1:T(1,128)S(1)}, s32[256,1]{0,1:T(1,128)}, u32[]{:S(2)}) copy-start(s32[256,1]{0,1:T(1,128)} %copy-done.32) | copy-start | bytes 3076
  240.9 8.5 %copy-start.35 = (s32[256,1]{0,1:T(1,128)S(1)}, s32[256,1]{0,1:T(1,128)}, u32[]{:S(2)}) copy-start(s32[256,1]{0,1:T(1,128)} %copy-done.34) | copy-start | bytes 3076
  240.9 9.0 %copy-start.19 = (s32[1,1,16,128]{3,2,1,0:T(8,128)S(1)}, s32[1,1,16,128]{3,2,1,0:T(8,128)}, u32[]{:S(2)}) copy-start(s32[1,1,16,128]{3,2,1,0:T(8,128)} %param.21) | copy-start | bytes 24580
  258.9 10.1 %copy-start.29 = (s32[256,1]{0,1:T(1,128)S(1)}, s32[256,1]{0,1:T(1,128)}, u32[]{:S(2)}) copy-start(s32[256,1]{0,1:T(1,128)} %copy-done.28) | copy-start | bytes 3076
  258.9 10.1 %copy-start.31 = (s32[256,1]{0,1:T(1,128)S(1)}, s32[256,1]{0,1:T(1,128)}, u32[]{:S(2)}) copy-start(s32[256,1]{0,1:T(1,128)} %copy-done.30) | copy-start | bytes 3076
  258.9 10.6 %copy-start.25 = (s32[256,1]{0,1:T(1,128)S(1)}, s32[256,1]{0,1:T(1,128)}, u32[]{:S(2)}) copy-start(s32[256,1]{0,1:T(1,128)} %copy-done.24) | copy-start | bytes 3076
  258.9 10.6 %copy-start.27 = (s32[256,1]{0,1:T(1,128)S(1)}, s32[256,1]{0,1:T(1,128)}, u32[]{:S(2)}) copy-start(s32[256,1]{0,1:T(1,128)} %copy-done.26) | copy-start | bytes 3076
  261.2 11.1 %copy-start.13 = (bf16[256,256]{1,0:T(8,128)(2,1)S(1)}, bf16[256,256]{1,0:T(8,128)(2,1)}, u32[]{:S(2)}) copy-start(bf16[256,256]{1,0:T(8,128)(2,1)} %param.18) | copy-start | bytes 393220
  261.2 21.7 %all-to-all-start = ((bf16[16,128,256]{2,1,0:T(8,128)(2,1)}), bf16[16,128,256]{2,1,0:T(8,128)(2,1)}, u32[]{:S(2)}, u32[]{:S(2)}) async-start(bf16[16,128,256]{2,1,0:T(8,128)(2,1)} %broadcast_select_fusion), calls=%async_computation.1 | async-start | bytes 2097152 | tf_op jit(solution)/shard_map/all_to_all | solution.py:60
  268.1 314.7 %all-reduce.5.cloned.1.call-start = ((), (), s32[]{:S(2)}) async-start(), calls=%async_computation.5 | async-start | bytes 1048576 | tf_op jit(solution)/shard_map/psum | solution.py:104
  313.9 12.5 %copy-start.45 = (pred[256]{0:T(512)(128)(4,1)S(1)}, pred[256]{0:T(512)(128)(4,1)}, u32[]{:S(2)}) copy-start(pred[256]{0:T(512)(128)(4,1)} %get-tuple-element.73) | copy-start | bytes 772
  313.9 12.5 %copy-start.46 = (pred[256]{0:T(512)(128)(4,1)S(1)}, pred[256]{0:T(512)(128)(4,1)}, u32[]{:S(2)}) copy-start(pred[256]{0:T(512)(128)(4,1)} %get-tuple-element.74) | copy-start | bytes 772
  313.9 12.5 %copy-start.47 = (pred[256]{0:T(512)(128)(4,1)S(1)}, pred[256]{0:T(512)(128)(4,1)}, u32[]{:S(2)}) copy-start(pred[256]{0:T(512)(128)(4,1)} %get-tuple-element.75) | copy-start | bytes 772
  313.9 12.5 %copy-start.48 = (pred[256]{0:T(512)(128)(4,1)S(1)}, pred[256]{0:T(512)(128)(4,1)}, u32[]{:S(2)}) copy-start(pred[256]{0:T(512)(128)(4,1)} %get-tuple-element.76) | copy-start | bytes 772
  329.3 347.9 %all-reduce.7.cloned.1.call-start = ((), (), s32[]{:S(2)}) async-start(), calls=%async_computation.6 | async-start | bytes 262144 | tf_op jit(solution)/shard_map/psum | solution.py:103
  (33 other events, 151.9 us)
Sparse Core Ops, SparseCore 0:
  131.1 66.7 reduce-scatter.1
  245.4 42.2 all-gather.1
  329.5 253.2 all-reduce.4
  586.5 90.7 all-reduce.6
where the time goes:
time: 700 us; the launch traced here: 690 us
  waiting for transfers between devices  353 us (50%)
  local copies, waits for them, and re-layouts  172 us (25%)
  other arithmetic  122 us (17%)
  starting transfers between devices  14.8 us (2%)
  between operations  14.7 us (2%)
  matrix products  13.2 us (2%)
    psum x1, waiting for transfers between devices, per_device(): lax.psum((local_w2_self, local_w2_neigh), ('feat', 'dom'))  248 us
    gather x10, local copies, waits for them, and re-layouts, per_device(): jnp.take(feature_table, neigh_lists[column], axis=1).astype(jnp.float32)  101 us
    psum x1, waiting for transfers between devices, per_device(): first_self, first_mean = lax.psum((first_self, first_mean), 'dom')  94.5 us
    scatter-add x15, other arithmetic, per_device(): slot_sum = slot_sum.at[where_in[:, column]].add(d_mean)  70.3 us
    gather x17, local copies, waits for them, and re-layouts, rows_of(): return jnp.take(source_table, index_rows, axis=0)  53.6 us
    unnamed x108, local copies, waits for them, and re-layouts  15.1 us
  transfers between devices with their start and end apart: 6, of which 4 were waited for; matrix products, arithmetic and copies ran while one was open for 25% of the time, Pallas kernels for 0%

commit v1 on v0

--- a/solution.py
+++ b/solution.py
@@ -101,7 +101,7 @@
     first_self = jnp.dot(left_self, piece, preferred_element_type=jnp.float32)
     first_mean = jnp.dot(left_mean, piece, preferred_element_type=jnp.float32)
     first_self, first_mean = lax.psum((first_self, first_mean), "dom")
-    second_self, second_mean = lax.psum((local_w2_self, local_w2_neigh), ("feat", "dom"))
+    second_self, second_mean = lax.psum(lax.psum((local_w2_self, local_w2_neigh), "feat"), "dom")
     return (layer_out[None, None], first_self, first_mean, second_self, second_mean)
 
 

time: 700 us -> 563 us (0.80)
  waiting for transfers between devices: 353 us -> 216 us
    psum x1, waiting for transfers between devices: 248 us -> 106 us  [per_device(): lax.psum((local_w2_self, local_w2_neigh), 'feat')]
    unnamed x108 -> x116, local copies, waits for them, and re-layouts: 15.1 us -> 15.1 us
  transfers between devices with their start and end apart: 6 -> 6, of which waited for: 4 -> 4; matrix products, arithmetic and copies ran while one was open for 25% -> 32% of each run, Pallas kernels for 0% -> 0%
where the time goes in v1:
time: 563 us; the launch traced here: 553 us
  waiting for transfers between devices  216 us (38%)
  local copies, waits for them, and re-layouts  171 us (30%)
  other arithmetic  124 us (22%)
  between operations  14.8 us (3%)
  starting transfers between devices  14.7 us (3%)
  matrix products  13.2 us (2%)
    psum x1, waiting for transfers between devices, per_device(): lax.psum((local_w2_self, local_w2_neigh), 'feat')  106 us
    gather x10, local copies, waits for them, and re-layouts, per_device(): jnp.take(feature_table, neigh_lists[column], axis=1).astype(jnp.float32)  101 us
    psum x1, waiting for transfers between devices, per_device(): first_self, first_mean = lax.psum((first_self, first_mean), 'dom')  99.1 us
    scatter-add x15, other arithmetic, per_device(): slot_sum = slot_sum.at[where_in[:, column]].add(d_mean)  70.3 us
    gather x17, local copies, waits for them, and re-layouts, rows_of(): return jnp.take(source_table, index_rows, axis=0)  52.9 us
    unnamed x116, local copies, waits for them, and re-layouts  15.1 us
  transfers between devices with their start and end apart: 6, of which 4 were waited for; matrix products, arithmetic and copies ran while one was open for 32% of the time, Pallas kernels for 0%

profile of v1, /device:TPU:2, one launch (start us, length us, event | category | flops | bytes accessed | tf_op | source)
XLA Modules:
  0.0 553.1 jit_solution(3701543779336192720)
XLA Ops:
  11.5 10.1 %gather_fusion.2 = bf16[4608,64]{1,0:T(8,128)(2,1)} fusion(bf16[64,9216]{0,1:T(8,128)(2,1)S(1)} %bitcast.99, s32[5120]{0:T(1024)S(1)} %pad_clamp_fusion.9), kind=kCustom, calls=%fused_computation.clone | custom fusion | bytes 1198080 | tf_op jit(solution)/shard_map/jit(_take)/gather | solution.py:42
  21.6 10.1 %gather_fusion.3 = bf16[4608,64]{1,0:T(8,128)(2,1)} fusion(bf16[64,9216]{0,1:T(8,128)(2,1)S(1)} %bitcast.100, s32[5120]{0:T(1024)S(1)} %pad_clamp_fusion.8), kind=kCustom, calls=%fused_computation.2.clone | custom fusion | bytes 1198080 | tf_op jit(solution)/shard_map/jit(_take)/gather | solution.py:42
  31.7 10.1 %gather_fusion.4 = bf16[4608,64]{1,0:T(8,128)(2,1)} fusion(bf16[64,9216]{0,1:T(8,128)(2,1)S(1)} %bitcast.101, s32[5120]{0:T(1024)S(1)} %pad_clamp_fusion.7), kind=kCustom, calls=%fused_computation.3.clone | custom fusion | bytes 1198080 | tf_op jit(solution)/shard_map/jit(_take)/gather | solution.py:42
  41.8 10.1 %gather_fusion.5 = bf16[4608,64]{1,0:T(8,128)(2,1)} fusion(bf16[64,9216]{0,1:T(8,128)(2,1)S(1)} %bitcast.102, s32[5120]{0:T(1024)S(1)} %pad_clamp_fusion.6), kind=kCustom, calls=%fused_computation.4.clone | custom fusion | bytes 1198080 | tf_op jit(solution)/shard_map/jit(_take)/gather | solution.py:42
  51.9 10.1 %gather_fusion.6 = bf16[4608,64]{1,0:T(8,128)(2,1)} fusion(bf16[64,9216]{0,1:T(8,128)(2,1)S(1)} %bitcast.103, s32[5120]{0:T(1024)S(1)} %pad_clamp_fusion.5), kind=kCustom, calls=%fused_computation.5.clone | custom fusion | bytes 1198080 | tf_op jit(solution)/shard_map/jit(_take)/gather | solution.py:42
  62.1 10.1 %gather_fusion.7 = bf16[4608,64]{1,0:T(8,128)(2,1)} fusion(bf16[64,9216]{0,1:T(8,128)(2,1)S(1)} %bitcast.104, s32[5120]{0:T(1024)S(1)} %pad_clamp_fusion.4), kind=kCustom, calls=%fused_computation.6.clone | custom fusion | bytes 1198080 | tf_op jit(solution)/shard_map/jit(_take)/gather | solution.py:42
  72.2 10.1 %gather_fusion.8 = bf16[4608,64]{1,0:T(8,128)(2,1)} fusion(bf16[64,9216]{0,1:T(8,128)(2,1)S(1)} %bitcast.105, s32[5120]{0:T(1024)S(1)} %pad_clamp_fusion.3), kind=kCustom, calls=%fused_computation.7.clone | custom fusion | bytes 1198080 | tf_op jit(solution)/shard_map/jit(_take)/gather | solution.py:42
  82.3 10.1 %gather_fusion.9 = bf16[4608,64]{1,0:T(8,128)(2,1)} fusion(bf16[64,9216]{0,1:T(8,128)(2,1)S(1)} %bitcast.106, s32[5120]{0:T(1024)S(1)} %pad_clamp_fusion.2), kind=kCustom, calls=%fused_computation.8.clone | custom fusion | bytes 1198080 | tf_op jit(solution)/shard_map/jit(_take)/gather | solution.py:42
  92.4 10.1 %gather_fusion.10 = bf16[4608,64]{1,0:T(8,128)(2,1)} fusion(bf16[64,9216]{0,1:T(8,128)(2,1)S(1)} %bitcast.107, s32[5120]{0:T(1024)S(1)} %pad_clamp_fusion.1), kind=kCustom, calls=%fused_computation.9.clone | custom fusion | bytes 1198080 | tf_op jit(solution)/shard_map/jit(_take)/gather | solution.py:42
  102.6 10.1 %gather_fusion.11 = bf16[4608,64]{1,0:T(8,128)(2,1)} fusion(bf16[64,9216]{0,1:T(8,128)(2,1)S(1)} %bitcast.108, s32[5120]{0:T(1024)S(1)} %pad_clamp_fusion), kind=kCustom, calls=%fused_computation.10.clone | custom fusion | bytes 1198080 | tf_op jit(solution)/shard_map/jit(_take)/gather | solution.py:42
  116.8 10.3 %multiply_convert_fusion = bf16[64,4608]{0,1:T(8,128)(2,1)S(1)} fusion(bf16[4608,64]{1,0:T(8,128)(2,1)} %gather_fusion.11, bf16[4608,64]{1,0:T(8,128)(2,1)S(1)} %copy-done.11, bf16[4608,64]{1,0:T(8,128)(2,1)S(1)} %copy-done.10, bf16[4608,64]{1,0:T(8,128)(2,1)S(1)} %copy-done.9, bf16[4608,64]{1,0:T(8,128)(2,1)S(1)} %copy-done.8, ...), kind=kLoop, calls=%fused_computation.45 | loop fusion | flops 9142272 | bytes 6534144 | tf_op jit(solution)/shard_map/convert_element_type | solution.py:43
  141.2 5.2 scatter_fusion.1
  151.1 4.8 scatter_fusion.3
  165.3 4.8 scatter_fusion.6
  170.1 4.8 scatter_fusion.7
  184.3 4.8 scatter_fusion.10
  189.1 4.9 scatter_fusion.11
  206.2 7.5 %all-to-all-start.1 = ((bf16[16,128,256]{2,1,0:T(8,128)(2,1)}), bf16[16,128,256]{2,1,0:T(8,128)(2,1)S(1)}, u32[]{:S(2)}, u32[]{:S(2)}) async-start(bf16[16,128,256]{2,1,0:T(8,128)(2,1)} %bitcast.53), calls=%async_computation.2 | async-start | bytes 2097152 | tf_op jit(solution)/shard_map/all_to_all | solution.py:90
  229.7 11.0 %scatter_custom_fusion.15 = f32[288,256]{1,0:T(8,128)S(1)} fusion(s32[2048]{0:T(1024)S(1)} %bitcast.115, bf16[2048,256]{1,0:T(8,128)(2,1)} %bitcast.111, f32[]{:T(128)} %constant.47.clone.1), kind=kCustom, calls=%fused_computation.46 | custom fusion | flops 1048576 | bytes 1343492 | tf_op jit(solution)/shard_map/scatter-add | solution.py:92
  250.5 9.0 %gather_fusion.1 = bf16[2048,256]{1,0:T(8,128)(2,1)} fusion(bf16[288,256]{1,0:T(8,128)(2,1)S(1)} %get-tuple-element.24, s32[2048]{0:T(1024)S(1)} %broadcast_clamp_fusion), kind=kCustom, calls=%fused_computation.26 | custom fusion | bytes 2105344 | tf_op jit(solution)/shard_map/jit(_take)/gather | solution.py:8
  261.8 6.8 %all-to-all-start = ((bf16[16,128,256]{2,1,0:T(8,128)(2,1)}), bf16[16,128,256]{2,1,0:T(8,128)(2,1)}, u32[]{:S(2)}, u32[]{:S(2)}) async-start(bf16[16,128,256]{2,1,0:T(8,128)(2,1)} %broadcast_select_fusion), calls=%async_computation.1 | async-start | bytes 2097152 | tf_op jit(solution)/shard_map/all_to_all | solution.py:60
  273.5 9.9 %all-to-all-done = bf16[16,128,256]{2,1,0:T(8,128)(2,1)} async-done(((bf16[16,128,256]{2,1,0:T(8,128)(2,1)}), bf16[16,128,256]{2,1,0:T(8,128)(2,1)}, u32[]{:S(2)}, u32[]{:S(2)}) %all-to-all-start) | async-done | bytes 1048608 | tf_op jit(solution)/shard_map/all_to_all | solution.py:60
  333.8 106.0 %all-reduce.7.cloned.1.call-done = (f32[256,256]{1,0:T(8,128)}, f32[256,256]{1,0:T(8,128)}) async-done(((f32[256,256]{1,0:T(8,128)}, f32[256,256]{1,0:T(8,128)}), (f32[256,256]{1,0:T(8,128)}, f32[256,256]{1,0:T(8,128)})) %all-reduce.7.cloned.1.call-update) | async-done | bytes 524304 | tf_op jit(solution)/shard_map/psum | solution.py:104
  440.9 99.1 %all-reduce.5.cloned.1.call-done = (f32[64,256]{1,0:T(8,128)}, f32[64,256]{1,0:T(8,128)}, f32[256,256]{1,0:T(8,128)}, f32[256,256]{1,0:T(8,128)}) async-done(((f32[64,256]{1,0:T(8,128)}, f32[64,256]{1,0:T(8,128)}, f32[256,256]{1,0:T(8,128)}, f32[256,256]{1,0:T(8,128)}), (f32[64,256]{1,0:T(8,128)}, f32[64,256]{1,0:T(8,128)}, f32[256,256]{1,0:T(8,128)}, f32[256,256]{1,0:T(8,128)})) %all-reduce.5.cloned.1.call-update) | async-done | bytes 655376 | tf_op jit(solution)/shard_map/psum | solution.py:103
  (242 shorter events, 148.4 us)
Async XLA Ops:
  7.2 125.6 %copy-start = (bf16[1,1,256,256]{3,2,1,0:T(8,128)(2,1)S(1)}, bf16[1,1,256,256]{3,2,1,0:T(8,128)(2,1)}, u32[]{:S(2)}) copy-start(bf16[1,1,256,256]{3,2,1,0:T(8,128)(2,1)} %param.25) | copy-start | bytes 393220
  7.2 236.3 %reduce-scatter.2.cloned.1.call-start = ((), (), s32[]{:S(2)}) async-start(), calls=%async_computation.3 | async-start | bytes 5013504 | tf_op jit(solution)/shard_map/reduce_scatter | solution.py:49
  102.5 10.1 %copy-start.17 = (bf16[64,256]{1,0:T(8,128)(2,1)S(1)}, bf16[64,256]{1,0:T(8,128)(2,1)}, u32[]{:S(2)}) copy-start(bf16[64,256]{1,0:T(8,128)(2,1)} %param.16) | copy-start | bytes 98308
  116.7 11.3 %copy-start.18 = (bf16[64,256]{1,0:T(8,128)(2,1)S(1)}, bf16[64,256]{1,0:T(8,128)(2,1)}, u32[]{:S(2)}) copy-start(bf16[64,256]{1,0:T(8,128)(2,1)} %param.17) | copy-start | bytes 98308
  206.2 22.5 %all-to-all-start.1 = ((bf16[16,128,256]{2,1,0:T(8,128)(2,1)}), bf16[16,128,256]{2,1,0:T(8,128)(2,1)S(1)}, u32[]{:S(2)}, u32[]{:S(2)}) async-start(bf16[16,128,256]{2,1,0:T(8,128)(2,1)} %bitcast.53), calls=%async_computation.2 | async-start | bytes 2097152 | tf_op jit(solution)/shard_map/all_to_all | solution.py:90
  213.7 115.5 %all-gather.2.cloned.1.call-start = ((), (), s32[]{:S(2)}) async-start(), calls=%async_computation.4 | async-start | bytes 2506752 | tf_op jit(solution)/shard_map/all_gather | solution.py:98
  240.9 9.6 %copy-start.19 = (s32[1,1,16,128]{3,2,1,0:T(8,128)S(1)}, s32[1,1,16,128]{3,2,1,0:T(8,128)}, u32[]{:S(2)}) copy-start(s32[1,1,16,128]{3,2,1,0:T(8,128)} %param.21) | copy-start | bytes 24580
  248.2 24.3 %copy-start.47 = (pred[256]{0:T(512)(128)(4,1)}, pred[256]{0:T(512)(128)(4,1)S(1)}, u32[]{:S(2)}) copy-start(pred[256]{0:T(512)(128)(4,1)S(1)} %compare_and_fusion.26) | copy-start | bytes 772
  259.5 10.0 %copy-start.33 = (s32[256,1]{0,1:T(1,128)S(1)}, s32[256,1]{0,1:T(1,128)}, u32[]{:S(2)}) copy-start(s32[256,1]{0,1:T(1,128)} %copy-done.32) | copy-start | bytes 3076
  259.5 10.0 %copy-start.35 = (s32[256,1]{0,1:T(1,128)S(1)}, s32[256,1]{0,1:T(1,128)}, u32[]{:S(2)}) copy-start(s32[256,1]{0,1:T(1,128)} %copy-done.34) | copy-start | bytes 3076
  259.5 10.5 %copy-start.29 = (s32[256,1]{0,1:T(1,128)S(1)}, s32[256,1]{0,1:T(1,128)}, u32[]{:S(2)}) copy-start(s32[256,1]{0,1:T(1,128)} %copy-done.28) | copy-start | bytes 3076
  259.5 10.5 %copy-start.31 = (s32[256,1]{0,1:T(1,128)S(1)}, s32[256,1]{0,1:T(1,128)}, u32[]{:S(2)}) copy-start(s32[256,1]{0,1:T(1,128)} %copy-done.30) | copy-start | bytes 3076
  259.5 11.1 %copy-start.25 = (s32[256,1]{0,1:T(1,128)S(1)}, s32[256,1]{0,1:T(1,128)}, u32[]{:S(2)}) copy-start(s32[256,1]{0,1:T(1,128)} %copy-done.24) | copy-start | bytes 3076
  259.5 11.1 %copy-start.27 = (s32[256,1]{0,1:T(1,128)S(1)}, s32[256,1]{0,1:T(1,128)}, u32[]{:S(2)}) copy-start(s32[256,1]{0,1:T(1,128)} %copy-done.26) | copy-start | bytes 3076
  261.8 21.6 %all-to-all-start = ((bf16[16,128,256]{2,1,0:T(8,128)(2,1)}), bf16[16,128,256]{2,1,0:T(8,128)(2,1)}, u32[]{:S(2)}, u32[]{:S(2)}) async-start(bf16[16,128,256]{2,1,0:T(8,128)(2,1)} %broadcast_select_fusion), calls=%async_computation.1 | async-start | bytes 2097152 | tf_op jit(solution)/shard_map/all_to_all | solution.py:60
  268.6 171.2 %all-reduce.7.cloned.1.call-start = ((), (), s32[]{:S(2)}) async-start(), calls=%async_computation.6 | async-start | bytes 1048576 | tf_op jit(solution)/shard_map/psum | solution.py:104
  313.6 12.5 %copy-start.49 = (pred[256]{0:T(512)(128)(4,1)S(1)}, pred[256]{0:T(512)(128)(4,1)}, u32[]{:S(2)}) copy-start(pred[256]{0:T(512)(128)(4,1)} %get-tuple-element.75) | copy-start | bytes 772
  313.6 12.5 %copy-start.50 = (pred[256]{0:T(512)(128)(4,1)S(1)}, pred[256]{0:T(512)(128)(4,1)}, u32[]{:S(2)}) copy-start(pred[256]{0:T(512)(128)(4,1)} %get-tuple-element.76) | copy-start | bytes 772
  313.6 12.5 %copy-start.51 = (pred[256]{0:T(512)(128)(4,1)S(1)}, pred[256]{0:T(512)(128)(4,1)}, u32[]{:S(2)}) copy-start(pred[256]{0:T(512)(128)(4,1)} %get-tuple-element.77) | copy-start | bytes 772
  313.7 12.5 %copy-start.52 = (pred[256]{0:T(512)(128)(4,1)S(1)}, pred[256]{0:T(512)(128)(4,1)}, u32[]{:S(2)}) copy-start(pred[256]{0:T(512)(128)(4,1)} %get-tuple-element.78) | copy-start | bytes 772
  329.1 210.9 %all-reduce.5.cloned.1.call-start = ((), (), s32[]{:S(2)}) async-start(), calls=%async_computation.5 | async-start | bytes 1310720 | tf_op jit(solution)/shard_map/psum | solution.py:103
  332.5 107.3 %copy-start.13 = (bf16[256,256]{1,0:T(8,128)(2,1)S(1)}, bf16[256,256]{1,0:T(8,128)(2,1)}, u32[]{:S(2)}) copy-start(bf16[256,256]{1,0:T(8,128)(2,1)} %param.18) | copy-start | bytes 393220
  332.5 107.3 %copy-start.48 = (pred[256]{0:T(512)(128)(4,1)S(1)}, pred[256]{0:T(512)(128)(4,1)}, u32[]{:S(2)}) copy-start(pred[256]{0:T(512)(128)(4,1)} %copy-done.47) | copy-start | bytes 772
  332.5 107.6 %copy-start.15 = (bf16[256,256]{1,0:T(8,128)(2,1)S(1)}, bf16[256,256]{1,0:T(8,128)(2,1)}, u32[]{:S(2)}) copy-start(bf16[256,256]{1,0:T(8,128)(2,1)} %param.19) | copy-start | bytes 393220
  (37 other events, 196.7 us)
Sparse Core Ops, SparseCore 0:
  131.1 66.7 reduce-scatter.1
  245.4 42.1 all-gather.1
  329.2 110.5 all-reduce.6
  444.3 95.7 all-reduce.4
